TPU v7x, 32 devices: a whole 2x2x4 slice. The times are simulated.
32 devices in a mesh: vec: 16 (over z, y, x), row: 2 (over core).
Axes of the slice: x: 2, y: 2, z: 4, core: 2. Of those that a mesh axis runs over, the one named last changes fastest.
Arguments:
- vectors: bfloat16 [2, 4096, 1024], P('row', 'vec'), may hold values from -6 to 6
- rotation: bfloat16 [1024, 1024], P(None, 'vec'), may hold values from -0.1875 to 0.1875
- blocks: bfloat16 [64, 8, 128, 128], P('row'), may hold values from -0.125 to 0.125
- column_blocks: int32 [64, 8], P('row'), may hold values from -2 to 65, as said below
Outputs:
- filtered: bfloat16 [2, 4096, 1024], P('row', 'vec')
Inputs may be any that keep to these rules, and one draw needn't show every extreme that they name: `column_blocks`: block row r of partition p = r // 32 lists 8 distinct column blocks between p * 32 - 2 and p * 32 + 33; the first block row of every partition lists the lowest of these and the last one the highest; column blocks outside 0 to 63 stand for zeros.
All inputs are finite; a program needn't handle non-finite values.
Results may differ from a plain program's by a relative error of at most 0.006.
Values may be sent and summed in bfloat16 or wider, within the bound.
No kernel may reach another device: no remote copies, remote signals or barrier semaphores. Data moves between devices by JAX's collectives and lax.ppermute only.
A program may use at most 64 MiB of HBM per device.

v0:
```python
import jax
import jax.numpy as jnp
from jax import lax
from jax.sharding import PartitionSpec as P

BS = 128
HB = 2
STEPS = 4
centre = 0.3
half_width = 1.2


def with_halo(block, sides, width):
    for axis, dim in sides:
        count = lax.axis_size(axis)
        forward = [(i, i + 1) for i in range(count - 1)]
        backward = [(target, source) for source, target in forward]
        low = lax.ppermute(
            lax.slice_in_dim(block, block.shape[dim] - width, None, axis=dim), axis, forward
        )
        high = lax.ppermute(lax.slice_in_dim(block, 0, width, axis=dim), axis, backward)
        block = jnp.concatenate([low, block, high], axis=dim)
    return block


def apply_matrix(operand, blocks, offsets):
    extended = with_halo(operand, (("row", 1),), HB * BS)
    stacked = extended.reshape(extended.shape[0], -1, BS)
    picked = stacked[:, offsets]
    product = jnp.einsum("rjab,krjb->kra", blocks, picked, preferred_element_type=jnp.float32)
    return product.reshape(extended.shape[0], -1)


def filter_panel(vec_panel, blocks, offsets):
    previous = vec_panel.astype(jnp.float32)
    current = (apply_matrix(vec_panel, blocks, offsets) - centre * previous) / half_width
    for turn_index in range(STEPS - 1):
        operand = current.astype(jnp.bfloat16)
        following = (
            2.0 * (apply_matrix(operand, blocks, offsets) - centre * current) / half_width
            - previous
        )
        previous = current
        current = following
    return current.astype(jnp.bfloat16)


def local(vectors, rotation, blocks, column_blocks):
    local_rows = vectors[0]
    offsets = column_blocks - (lax.axis_index("row") * column_blocks.shape[0] - HB)
    contract = (((0,), (1,)), ((), ()))
    rotated = lax.dot_general(
        lax.all_gather(rotation, "vec", axis=1, tiled=True),
        local_rows,
        contract,
        preferred_element_type=jnp.float32,
    ).astype(jnp.bfloat16)
    vec_panel = lax.all_to_all(rotated, "vec", split_axis=0, concat_axis=1, tiled=True)
    filtered = filter_panel(vec_panel, blocks, offsets)
    returned = lax.all_to_all(filtered, "vec", split_axis=1, concat_axis=0, tiled=True)
    return jnp.transpose(returned)[None]


def solution(mesh):
    placed = (P("row", "vec", None), P(None, "vec"), P("row", None, None, None), P("row", None))
    return jax.shard_map(
        local, mesh=mesh, in_specs=placed, out_specs=P("row", "vec", None), check_vma=False
    )
```

profile of v0, /device:TPU:0, one launch (start us, length us, event | category | flops | bytes accessed | tf_op | source)
XLA Modules:
  0.0 203.2 jit_solution(18180730329563429137)
XLA Ops:
  7.3 66.0 %all-gather.2.cloned.1.call-done = bf16[1024,1024]{0,1:T(8,128)(2,1)} async-done(((bf16[1024,64]{0,1:T(8,128)(2,1)}), bf16[1024,1024]{0,1:T(8,128)(2,1)}) %all-gather.2.cloned.1.call-update) | async-done | bytes 2097168 | tf_op jit(solution)/shard_map/all_gather | solution.py:53
  73.2 3.1 %convolution_convert_fusion = bf16[1024,256]{1,0:T(8,128)(2,1)} fusion(bf16[1024,1024]{0,1:T(8,128)(2,1)} %all-gather.2.cloned.1.call-done, bf16[1,256,1024]{2,1,0:T(8,128)(2,1)S(1)} %copy-done), kind=kOutput, calls=%fused_computation.9 | convolution fusion | flops 537133056 | bytes 3145728 | tf_op jit(solution)/shard_map/dot_general | solution.py:52
  76.4 4.4 %all-to-all-start = ((bf16[16,64,256]{2,1,0:T(8,128)(2,1)}), bf16[16,64,256]{2,1,0:T(8,128)(2,1)S(1)}, u32[]{:S(2)}, u32[]{:S(2)}) async-start(bf16[16,64,256]{2,1,0:T(8,128)(2,1)} %bitcast.1), calls=%async_computation | async-start | bytes 1048576 | tf_op jit(solution)/shard_map/all_to_all | solution.py:58
  81.0 14.0 %all-to-all-done = bf16[16,64,256]{2,1,0:T(8,128)(2,1)S(1)} async-done(((bf16[16,64,256]{2,1,0:T(8,128)(2,1)}), bf16[16,64,256]{2,1,0:T(8,128)(2,1)S(1)}, u32[]{:S(2)}, u32[]{:S(2)}) %all-to-all-start) | async-done | bytes 524320 | tf_op jit(solution)/shard_map/all_to_all | solution.py:58
  96.3 1.3 collective-permute-start.1
  97.7 1.8 collective-permute-done.1
  99.6 3.0 %gather_fusion = bf16[256,64,128]{2,1,0:T(8,128)(2,1)} fusion(bf16[64,36,128]{2,0,1:T(8,128)(2,1)S(1)} %copy_bitcast_fusion.3, s32[1024]{0:T(1024)S(1)} %pad_clamp_fusion), kind=kCustom, calls=%fused_computation | custom fusion | bytes 8389632 | tf_op jit(solution)/shard_map/gather | solution.py:29
  102.7 7.6 %fusion.12 = f32[32,64,128,1]{2,1,3,0:T(8,128)S(1)} fusion(bf16[64,32,8,128]{3,0,2,1:T(8,128)(2,1)} %bitcast.117, bf16[32,8,128,128]{3,2,1,0:T(8,128)(2,1)} %param.6), kind=kOutput, calls=%fused_computation.36 | convolution fusion | flops 536870912 | bytes 13631488 | tf_op jit(solution)/shard_map/rjab,krjb->kra/dot_general | solution.py:30
  110.5 2.1 %collective-permute-start.2 = (bf16[64,256]{1,0:T(8,128)(2,1)S(1)}, bf16[64,256]{1,0:T(8,128)(2,1)S(1)}, u32[]{:S(2)}, u32[]{:S(2)}) collective-permute-start(bf16[64,256]{1,0:T(8,128)(2,1)S(1)} %get-tuple-element.9), channel_id=1, source_target_pairs={{0,1},{2,3},{4,5},{6,7},{8,9},{10,11},{12,13},{14,15},{16,17},{18,... | collective-permute-start | bytes 98312 | tf_op jit(solution)/shard_map/ppermute | solution.py:18
  112.5 1.3 collective-permute-start.3
  113.8 1.8 collective-permute-done.3
  115.8 3.0 %gather_fusion.1 = bf16[256,64,128]{2,1,0:T(8,128)(2,1)} fusion(bf16[64,36,128]{2,0,1:T(8,128)(2,1)S(1)} %copy_bitcast_fusion.2, s32[1024]{0:T(1024)S(1)} %pad_clamp_fusion), kind=kCustom, calls=%fused_computation.1 | custom fusion | bytes 8389632 | tf_op jit(solution)/shard_map/gather | solution.py:29
  118.8 7.6 %fusion.13 = f32[32,64,128,1]{2,1,3,0:T(8,128)S(1)} fusion(bf16[64,32,8,128]{3,0,2,1:T(8,128)(2,1)} %bitcast.118, bf16[32,8,128,128]{3,2,1,0:T(8,128)(2,1)} %param.6), kind=kOutput, calls=%fused_computation.37 | convolution fusion | flops 536870912 | bytes 13631488 | tf_op jit(solution)/shard_map/rjab,krjb->kra/dot_general | solution.py:30
  126.8 2.1 %collective-permute-start.4 = (bf16[64,256]{1,0:T(8,128)(2,1)S(1)}, bf16[64,256]{1,0:T(8,128)(2,1)S(1)}, u32[]{:S(2)}, u32[]{:S(2)}) collective-permute-start(bf16[64,256]{1,0:T(8,128)(2,1)S(1)} %get-tuple-element.7), channel_id=1, source_target_pairs={{0,1},{2,3},{4,5},{6,7},{8,9},{10,11},{12,13},{14,15},{16,17},{18,... | collective-permute-start | bytes 98312 | tf_op jit(solution)/shard_map/ppermute | solution.py:18
  128.9 1.3 collective-permute-start.5
  130.2 1.8 collective-permute-done.5
  132.1 3.0 %gather_fusion.2 = bf16[256,64,128]{2,1,0:T(8,128)(2,1)} fusion(bf16[64,36,128]{2,0,1:T(8,128)(2,1)S(1)} %copy_bitcast_fusion.1, s32[1024]{0:T(1024)S(1)} %pad_clamp_fusion), kind=kCustom, calls=%fused_computation.2 | custom fusion | bytes 8389632 | tf_op jit(solution)/shard_map/gather | solution.py:29
  135.2 7.6 %fusion.14 = f32[32,64,128,1]{2,1,3,0:T(8,128)S(1)} fusion(bf16[64,32,8,128]{3,0,2,1:T(8,128)(2,1)} %bitcast.119, bf16[32,8,128,128]{3,2,1,0:T(8,128)(2,1)} %param.6), kind=kOutput, calls=%fused_computation.38 | convolution fusion | flops 536870912 | bytes 13631488 | tf_op jit(solution)/shard_map/rjab,krjb->kra/dot_general | solution.py:30
  143.8 2.1 %collective-permute-start.6 = (bf16[64,256]{1,0:T(8,128)(2,1)S(1)}, bf16[64,256]{1,0:T(8,128)(2,1)S(1)}, u32[]{:S(2)}, u32[]{:S(2)}) collective-permute-start(bf16[64,256]{1,0:T(8,128)(2,1)S(1)} %get-tuple-element.5), channel_id=1, source_target_pairs={{0,1},{2,3},{4,5},{6,7},{8,9},{10,11},{12,13},{14,15},{16,17},{18,... | collective-permute-start | bytes 98312 | tf_op jit(solution)/shard_map/ppermute | solution.py:18
  145.9 1.5 collective-permute-start.7
  147.4 1.6 copy.24
  149.0 2.6 %reshape.50 = f32[64,16,256]{2,1,0:T(8,128)} reshape(f32[64,32,128]{2,1,0:T(8,128)} %copy.24) | data formatting | bytes 2097152 | tf_op jit(solution)/shard_map/reshape | solution.py:31
  151.6 1.6 copy.26
  153.2 1.5 reshape.49
  154.7 1.6 copy.28
  156.3 2.5 %reshape.48 = f32[64,16,256]{2,1,0:T(8,128)} reshape(f32[64,32,128]{2,1,0:T(8,128)} %copy.28) | data formatting | bytes 2097152 | tf_op jit(solution)/shard_map/reshape | solution.py:31
  159.0 3.0 %gather_fusion.3 = bf16[256,64,128]{2,1,0:T(8,128)(2,1)} fusion(bf16[64,36,128]{2,0,1:T(8,128)(2,1)S(1)} %copy_bitcast_fusion, s32[1024]{0:T(1024)S(1)} %pad_clamp_fusion), kind=kCustom, calls=%fused_computation.3 | custom fusion | bytes 8389632 | tf_op jit(solution)/shard_map/gather | solution.py:29
  162.1 7.6 %convolution_bitcast_fusion = f32[64,32,128]{2,0,1:T(8,128)S(1)} fusion(bf16[64,32,8,128]{3,0,2,1:T(8,128)(2,1)} %bitcast.116, bf16[32,8,128,128]{3,2,1,0:T(8,128)(2,1)} %param.6), kind=kOutput, calls=%fused_computation.4 | convolution fusion | flops 536870912 | bytes 13631488 | tf_op jit(solution)/shard_map/rjab,krjb->kra/dot_general | solution.py:30
  169.7 1.6 copy.30
  171.3 2.5 %reshape.47 = f32[64,16,256]{2,1,0:T(8,128)} reshape(f32[64,32,128]{2,1,0:T(8,128)} %copy.30) | data formatting | bytes 2097152 | tf_op jit(solution)/shard_map/reshape | solution.py:31
  173.8 2.4 %subtract_convert_fusion = bf16[64,16,256]{2,1,0:T(8,128)(2,1)S(1)} fusion(f32[64,16,256]{2,1,0:T(8,128)} %reshape.47, f32[64,16,256]{2,1,0:T(8,128)} %reshape.48, f32[64,16,256]{2,1,0:T(8,128)S(1)} %reshape.49, f32[64,16,256]{2,1,0:T(8,128)S(1)} %copy-done.8, bf16[16,64,256]{2,1,0:T(8,128)(2,1)S(1)} %copy-done.7), kind=kLoop, calls=%fused_computation.18 | loop fusion | flops 4456448 | bytes 5242880 | tf_op jit(solution)/shard_map/convert_element_type | solution.py:45
  176.3 19.0 %all_to_all.35 = bf16[64,16,256]{2,0,1:T(8,128)(2,1)S(1)} all-to-all(bf16[64,16,256]{2,0,1:T(8,128)(2,1)S(1)} %copy.34), channel_id=1, replica_groups=mesh['vec'=16,'row'=2] {'vec'}, dimensions={1} | all-to-all | bytes 1048576 | tf_op jit(solution)/shard_map/all_to_all | solution.py:60
  (50 shorter events, 5.5 us)
Async XLA Ops:
  6.5 66.7 %copy-start = (bf16[1,256,1024]{2,1,0:T(8,128)(2,1)S(1)}, bf16[1,256,1024]{2,1,0:T(8,128)(2,1)}, u32[]{:S(2)}) copy-start(bf16[1,256,1024]{2,1,0:T(8,128)(2,1)} %param.4) | copy-start | bytes 1572868
  6.5 74.3 %copy-start.11 = (s32[32,8]{0,1:T(8,128)S(1)}, s32[32,8]{0,1:T(8,128)}, u32[]{:S(2)}) copy-start(s32[32,8]{0,1:T(8,128)} %param.7) | copy-start | bytes 3076
  6.5 66.7 %all-gather.2.cloned.1.call-start = ((), (), s32[]{:S(2)}) async-start(), calls=%async_computation.2 | async-start | bytes 2228224 | tf_op jit(solution)/shard_map/all_gather | solution.py:53
  76.4 18.6 %all-to-all-start = ((bf16[16,64,256]{2,1,0:T(8,128)(2,1)}), bf16[16,64,256]{2,1,0:T(8,128)(2,1)S(1)}, u32[]{:S(2)}, u32[]{:S(2)}) async-start(bf16[16,64,256]{2,1,0:T(8,128)(2,1)} %bitcast.1), calls=%async_computation | async-start | bytes 1048576 | tf_op jit(solution)/shard_map/all_to_all | solution.py:58
  95.0 2.7 %copy-start.6 = (bf16[16,64,256]{2,1,0:T(8,128)(2,1)}, bf16[16,64,256]{2,1,0:T(8,128)(2,1)S(1)}, u32[]{:S(2)}) copy-start(bf16[16,64,256]{2,1,0:T(8,128)(2,1)S(1)} %all-to-all-done) | copy-start | bytes 1572868
  95.0 15.2 %copy-start.1 = (bf16[8,8,16,256]{3,1,2,0:T(8,128)(2,1)}, bf16[8,8,16,256]{3,1,2,0:T(8,128)(2,1)S(1)}, u32[]{:S(2)}) copy-start(bf16[8,8,16,256]{3,1,2,0:T(8,128)(2,1)S(1)} %copy.47) | copy-start | bytes 1572868
  95.0 2.6 %collective-permute-start = (bf16[64,256]{1,0:T(8,128)(2,1)S(1)}, bf16[64,256]{1,0:T(8,128)(2,1)S(1)}, u32[]{:S(2)}, u32[]{:S(2)}) collective-permute-start(bf16[64,256]{1,0:T(8,128)(2,1)S(1)} %get-tuple-element.11), channel_id=1, source_target_pairs={{0,1},{2,3},{4,5},{6,7},{8,9},{10,11},{12,13},{14,15},{16,17},{18,... | collective-permute-start | bytes 98312 | tf_op jit(solution)/shard_map/ppermute | solution.py:18
  96.3 3.1 %collective-permute-start.1 = (bf16[64,256]{1,0:T(8,128)(2,1)S(1)}, bf16[64,256]{1,0:T(8,128)(2,1)S(1)}, u32[]{:S(2)}, u32[]{:S(2)}) collective-permute-start(bf16[64,256]{1,0:T(8,128)(2,1)S(1)} %get-tuple-element.12), channel_id=1, source_target_pairs={{1,0},{3,2},{5,4},{7,6},{9,8},{11,10},{13,12},{15,14},{17,16},{19,... | collective-permute-start | bytes 98312 | tf_op jit(solution)/shard_map/ppermute | solution.py:21
  110.5 3.4 %collective-permute-start.2 = (bf16[64,256]{1,0:T(8,128)(2,1)S(1)}, bf16[64,256]{1,0:T(8,128)(2,1)S(1)}, u32[]{:S(2)}, u32[]{:S(2)}) collective-permute-start(bf16[64,256]{1,0:T(8,128)(2,1)S(1)} %get-tuple-element.9), channel_id=1, source_target_pairs={{0,1},{2,3},{4,5},{6,7},{8,9},{10,11},{12,13},{14,15},{16,17},{18,... | collective-permute-start | bytes 98312 | tf_op jit(solution)/shard_map/ppermute | solution.py:18
  112.5 3.1 %collective-permute-start.3 = (bf16[64,256]{1,0:T(8,128)(2,1)S(1)}, bf16[64,256]{1,0:T(8,128)(2,1)S(1)}, u32[]{:S(2)}, u32[]{:S(2)}) collective-permute-start(bf16[64,256]{1,0:T(8,128)(2,1)S(1)} %get-tuple-element.10), channel_id=1, source_target_pairs={{1,0},{3,2},{5,4},{7,6},{9,8},{11,10},{13,12},{15,14},{17,16},{19,... | collective-permute-start | bytes 98312 | tf_op jit(solution)/shard_map/ppermute | solution.py:21
  118.8 7.7 %copy-start.2 = (bf16[8,8,16,256]{3,1,2,0:T(8,128)(2,1)S(1)}, bf16[8,8,16,256]{3,1,2,0:T(8,128)(2,1)}, u32[]{:S(2)}) copy-start(bf16[8,8,16,256]{3,1,2,0:T(8,128)(2,1)} %copy-done.1) | copy-start | bytes 1572868
  126.8 3.4 %collective-permute-start.4 = (bf16[64,256]{1,0:T(8,128)(2,1)S(1)}, bf16[64,256]{1,0:T(8,128)(2,1)S(1)}, u32[]{:S(2)}, u32[]{:S(2)}) collective-permute-start(bf16[64,256]{1,0:T(8,128)(2,1)S(1)} %get-tuple-element.7), channel_id=1, source_target_pairs={{0,1},{2,3},{4,5},{6,7},{8,9},{10,11},{12,13},{14,15},{16,17},{18,... | collective-permute-start | bytes 98312 | tf_op jit(solution)/shard_map/ppermute | solution.py:18
  128.9 3.1 %collective-permute-start.5 = (bf16[64,256]{1,0:T(8,128)(2,1)S(1)}, bf16[64,256]{1,0:T(8,128)(2,1)S(1)}, u32[]{:S(2)}, u32[]{:S(2)}) collective-permute-start(bf16[64,256]{1,0:T(8,128)(2,1)S(1)} %get-tuple-element.8), channel_id=1, source_target_pairs={{1,0},{3,2},{5,4},{7,6},{9,8},{11,10},{13,12},{15,14},{17,16},{19,... | collective-permute-start | bytes 98312 | tf_op jit(solution)/shard_map/ppermute | solution.py:21
  135.2 7.7 %copy-start.3 = (bf16[8,8,16,256]{3,1,2,0:T(8,128)(2,1)S(1)}, bf16[8,8,16,256]{3,1,2,0:T(8,128)(2,1)}, u32[]{:S(2)}) copy-start(bf16[8,8,16,256]{3,1,2,0:T(8,128)(2,1)} %copy-done.1) | copy-start | bytes 1572868
  142.8 1.0 copy-start.4
  143.8 3.6 %copy-start.9 = (bf16[64,4096]{1,0:T(8,128)(2,1)}, bf16[64,4096]{1,0:T(8,128)(2,1)S(1)}, u32[]{:S(2)}) copy-start(bf16[64,4096]{1,0:T(8,128)(2,1)S(1)} %fusion.4) | copy-start | bytes 1572868
  143.8 15.0 %collective-permute-start.6 = (bf16[64,256]{1,0:T(8,128)(2,1)S(1)}, bf16[64,256]{1,0:T(8,128)(2,1)S(1)}, u32[]{:S(2)}, u32[]{:S(2)}) collective-permute-start(bf16[64,256]{1,0:T(8,128)(2,1)S(1)} %get-tuple-element.5), channel_id=1, source_target_pairs={{0,1},{2,3},{4,5},{6,7},{8,9},{10,11},{12,13},{14,15},{16,17},{18,... | collective-permute-start | bytes 98312 | tf_op jit(solution)/shard_map/ppermute | solution.py:18
  145.9 12.9 %collective-permute-start.7 = (bf16[64,256]{1,0:T(8,128)(2,1)S(1)}, bf16[64,256]{1,0:T(8,128)(2,1)S(1)}, u32[]{:S(2)}, u32[]{:S(2)}) collective-permute-start(bf16[64,256]{1,0:T(8,128)(2,1)S(1)} %get-tuple-element.6), channel_id=1, source_target_pairs={{1,0},{3,2},{5,4},{7,6},{9,8},{11,10},{13,12},{15,14},{17,16},{19,... | collective-permute-start | bytes 98312 | tf_op jit(solution)/shard_map/ppermute | solution.py:21
  149.0 5.7 %copy-start.5 = (f32[32,64,128,1]{2,1,3,0:T(8,128)S(1)}, f32[32,64,128,1]{2,1,3,0:T(8,128)}, u32[]{:S(2)}) copy-start(f32[32,64,128,1]{2,1,3,0:T(8,128)} %copy-done.4) | copy-start | bytes 3145732
  151.6 7.2 %copy-start.10 = (bf16[64,4096]{1,0:T(8,128)(2,1)S(1)}, bf16[64,4096]{1,0:T(8,128)(2,1)}, u32[]{:S(2)}) copy-start(bf16[64,4096]{1,0:T(8,128)(2,1)} %copy-done.9) | copy-start | bytes 1572868
  169.7 4.1 %copy-start.7 = (bf16[16,64,256]{2,1,0:T(8,128)(2,1)S(1)}, bf16[16,64,256]{2,1,0:T(8,128)(2,1)}, u32[]{:S(2)}) copy-start(bf16[16,64,256]{2,1,0:T(8,128)(2,1)} %copy-done.6) | copy-start | bytes 1572868
  169.7 4.1 %copy-start.8 = (f32[64,16,256]{2,1,0:T(8,128)S(1)}, f32[64,16,256]{2,1,0:T(8,128)}, u32[]{:S(2)}) copy-start(f32[64,16,256]{2,1,0:T(8,128)} %reshape.50) | copy-start | bytes 3145732
Sparse Core Ops, SparseCore 0:
  10.1 63.0 all-gather.1
where the time goes:
time: 204 us; the launch traced here: 203 us
  waiting for transfers between devices  86 us (42%)
  matrix products  33.6 us (16%)
  local copies, waits for them, and re-layouts  29.7 us (15%)
  blocking collectives  19 us (9%)
  starting transfers between devices  17.3 us (8%)
  between operations  13.7 us (7%)
  other arithmetic  3.9 us (2%)
    all_gather x1, waiting for transfers between devices, local(): lax.all_gather(rotation, 'vec', axis=1, tiled=True)  66 us
    dot_general x4, matrix products, apply_matrix(): jnp.einsum('rjab,krjb->kra', blocks, picked, preferred_element_type=jnp.f...  30.5 us
    all_to_all x1, blocking collectives, local(): lax.all_to_all(filtered, 'vec', split_axis=1, concat_axis=0, tiled=True)  19 us
    all_to_all x1, waiting for transfers between devices, local(): lax.all_to_all(rotated, 'vec', split_axis=0, concat_axis=1, tiled=True)  14 us
    gather x4, local copies, waits for them, and re-layouts, apply_matrix(): picked = stacked[:, offsets]  12.2 us
    reshape x4, local copies, waits for them, and re-layouts, apply_matrix(): return product.reshape(extended.shape[0], -1)  9.18 us
    ppermute x4, starting transfers between devices, with_halo(): lax.ppermute(lax.slice_in_dim(block, block.shape[dim] - width, None, axis...  7.49 us
    transpose x4, local copies, waits for them, and re-layouts, apply_matrix(): jnp.einsum('rjab,krjb->kra', blocks, picked, preferred_element_type=jnp.f...  6.33 us
  transfers between devices with their start and end apart: 10, of which 5 were waited for; matrix products, arithmetic and copies ran while one was open for 6% of the time, Pallas kernels for 0%

commit v1 on v0

--- a/solution.py
+++ b/solution.py
@@ -2,6 +2,7 @@
 import jax.numpy as jnp
 from jax import lax
 from jax.sharding import PartitionSpec as P
+from jax.lax import all_to_all, axis_size
 
 BS = 128
 HB = 2
@@ -46,6 +47,14 @@
 
 
 def local(vectors, rotation, blocks, column_blocks):
+
+    def pools_note(vec):
+        left_arr = axis_size("vec")
+        formed = jnp.split(vec, left_arr, axis=1)
+        y2 = jnp.stack(formed)
+        aux = all_to_all(y2, "vec", 0, 0)
+        return jnp.concatenate(aux, axis=0)
+
     local_rows = vectors[0]
     offsets = column_blocks - (lax.axis_index("row") * column_blocks.shape[0] - HB)
     contract = (((0,), (1,)), ((), ()))
@@ -57,7 +66,7 @@
     ).astype(jnp.bfloat16)
     vec_panel = lax.all_to_all(rotated, "vec", split_axis=0, concat_axis=1, tiled=True)
     filtered = filter_panel(vec_panel, blocks, offsets)
-    returned = lax.all_to_all(filtered, "vec", split_axis=1, concat_axis=0, tiled=True)
+    returned = pools_note(filtered)
     return jnp.transpose(returned)[None]
 
 

time: 204 us -> 188 us (0.922)
  local copies, waits for them, and re-layouts: 29.7 us -> 13.5 us
    reshape x4 -> x0, local copies, waits for them, and re-layouts: 9.18 us -> none  [apply_matrix(): return product.reshape(extended.shape[0], -1)]
    transpose x4 -> x0, local copies, waits for them, and re-layouts: 6.33 us -> none  [apply_matrix(): jnp.einsum('rjab,krjb->kra', blocks, picked, preferred_element_type=jnp.f...]
  transfers between devices with their start and end apart: 10 -> 10, of which waited for: 5 -> 6; matrix products, arithmetic and copies ran while one was open for 6% -> 0% of each run, Pallas kernels for 0% -> 0%
where the time goes in v1:
time: 188 us; the launch traced here: 187 us
  waiting for transfers between devices  87.6 us (47%)
  matrix products  33.7 us (18%)
  blocking collectives  19.1 us (10%)
  starting transfers between devices  17.3 us (9%)
  between operations  13.8 us (7%)
  local copies, waits for them, and re-layouts  13.5 us (7%)
  other arithmetic  2.12 us (1%)
    all_gather x1, waiting for transfers between devices, local(): lax.all_gather(rotation, 'vec', axis=1, tiled=True)  66 us
    dot_general x4, matrix products, apply_matrix(): jnp.einsum('rjab,krjb->kra', blocks, picked, preferred_element_type=jnp.f...  30.6 us
    all_to_all x1, blocking collectives, pools_note(): aux = all_to_all(y2, 'vec', 0, 0)  19.1 us
    all_to_all x1, waiting for transfers between devices, local(): lax.all_to_all(rotated, 'vec', split_axis=0, concat_axis=1, tiled=True)  14 us
    gather x4, local copies, waits for them, and re-layouts, apply_matrix(): picked = stacked[:, offsets]  12.1 us
    ppermute x4, starting transfers between devices, with_halo(): lax.ppermute(lax.slice_in_dim(block, block.shape[dim] - width, None, axis...  7.5 us
    ppermute x4, waiting for transfers between devices, with_halo(): lax.ppermute(lax.slice_in_dim(block, 0, width, axis=dim), axis, backward)  6.95 us
    ppermute x4, starting transfers between devices, with_halo(): lax.ppermute(lax.slice_in_dim(block, 0, width, axis=dim), axis, backward)  5.35 us
  transfers between devices with their start and end apart: 10, of which 6 were waited for; matrix products, arithmetic and copies ran while one was open for 0% of the time, Pallas kernels for 0%

profile of v1, /device:TPU:0, one launch (start us, length us, event | category | flops | bytes accessed | tf_op | source)
XLA Modules:
  0.0 187.1 jit_solution(857645403118411049)
XLA Ops:
  6.5 0.7 all-gather.2.cloned.1.call-update
  7.3 66.0 %all-gather.2.cloned.1.call-done = bf16[1024,1024]{0,1:T(8,128)(2,1)} async-done(((bf16[1024,64]{0,1:T(8,128)(2,1)}), bf16[1024,1024]{0,1:T(8,128)(2,1)}) %all-gather.2.cloned.1.call-update) | async-done | bytes 2097168 | tf_op jit(solution)/shard_map/all_gather | solution.py:62
  73.2 3.1 %convolution_convert_fusion = bf16[1024,256]{1,0:T(8,128)(2,1)} fusion(bf16[1024,1024]{0,1:T(8,128)(2,1)} %all-gather.2.cloned.1.call-done, bf16[1,256,1024]{2,1,0:T(8,128)(2,1)S(1)} %copy-done), kind=kOutput, calls=%fused_computation.10 | convolution fusion | flops 537133056 | bytes 3145728 | tf_op jit(solution)/shard_map/dot_general | solution.py:61
  76.4 4.4 %all-to-all-start = ((bf16[16,64,256]{2,1,0:T(8,128)(2,1)}), bf16[16,64,256]{2,1,0:T(8,128)(2,1)S(1)}, u32[]{:S(2)}, u32[]{:S(2)}) async-start(bf16[16,64,256]{2,1,0:T(8,128)(2,1)} %bitcast.1), calls=%async_computation | async-start | bytes 1048576 | tf_op jit(solution)/shard_map/all_to_all | solution.py:67
  81.0 14.0 %all-to-all-done = bf16[16,64,256]{2,1,0:T(8,128)(2,1)S(1)} async-done(((bf16[16,64,256]{2,1,0:T(8,128)(2,1)}), bf16[16,64,256]{2,1,0:T(8,128)(2,1)S(1)}, u32[]{:S(2)}, u32[]{:S(2)}) %all-to-all-start) | async-done | bytes 524320 | tf_op jit(solution)/shard_map/all_to_all | solution.py:67
  95.0 1.3 collective-permute-start
  96.3 1.3 collective-permute-start.1
  97.7 1.8 collective-permute-done.1
  99.4 0.2 copy_bitcast_fusion.3
  99.6 3.0 %gather_fusion = bf16[256,64,128]{2,1,0:T(8,128)(2,1)} fusion(bf16[64,36,128]{2,0,1:T(8,128)(2,1)S(1)} %copy_bitcast_fusion.3, s32[1024]{0:T(1024)S(1)} %pad_clamp_fusion), kind=kCustom, calls=%fused_computation | custom fusion | bytes 8389632 | tf_op jit(solution)/shard_map/gather | solution.py:30
  102.6 7.6 %convolution_bitcast_fusion.3 = f32[32,8,8,128]{3,2,1,0:T(8,128)S(1)} fusion(bf16[64,32,8,128]{3,0,2,1:T(8,128)(2,1)} %bitcast.196, bf16[32,8,128,128]{3,2,1,0:T(8,128)(2,1)} %param.6), kind=kOutput, calls=%fused_computation.7 | convolution fusion | flops 536870912 | bytes 13631488 | tf_op jit(solution)/shard_map/rjab,krjb->kra/dot_general | solution.py:31
  110.2 0.2 multiply_convert_fusion
  110.4 2.1 %collective-permute-start.2 = (bf16[64,256]{1,0:T(8,128)(2,1)S(1)}, bf16[64,256]{1,0:T(8,128)(2,1)S(1)}, u32[]{:S(2)}, u32[]{:S(2)}) collective-permute-start(bf16[64,256]{1,0:T(8,128)(2,1)S(1)} %get-tuple-element.9), channel_id=1, source_target_pairs={{0,1},{2,3},{4,5},{6,7},{8,9},{10,11},{12,13},{14,15},{16,17},{18,... | collective-permute-start | bytes 98312 | tf_op jit(solution)/shard_map/ppermute | solution.py:19
  112.5 1.3 collective-permute-start.3
  113.8 1.8 collective-permute-done.3
  115.8 3.0 %gather_fusion.1 = bf16[256,64,128]{2,1,0:T(8,128)(2,1)} fusion(bf16[64,36,128]{2,0,1:T(8,128)(2,1)S(1)} %copy_bitcast_fusion.2, s32[1024]{0:T(1024)S(1)} %pad_clamp_fusion), kind=kCustom, calls=%fused_computation.1 | custom fusion | bytes 8389632 | tf_op jit(solution)/shard_map/gather | solution.py:30
  118.8 7.6 %convolution_bitcast_fusion.2 = f32[32,8,8,128]{3,2,1,0:T(8,128)S(1)} fusion(bf16[64,32,8,128]{3,0,2,1:T(8,128)(2,1)} %bitcast.197, bf16[32,8,128,128]{3,2,1,0:T(8,128)(2,1)} %param.6), kind=kOutput, calls=%fused_computation.6 | convolution fusion | flops 536870912 | bytes 13631488 | tf_op jit(solution)/shard_map/rjab,krjb->kra/dot_general | solution.py:31
  126.4 0.3 fusion.25
  126.7 2.1 %collective-permute-start.4 = (bf16[64,256]{1,0:T(8,128)(2,1)S(1)}, bf16[64,256]{1,0:T(8,128)(2,1)S(1)}, u32[]{:S(2)}, u32[]{:S(2)}) collective-permute-start(bf16[64,256]{1,0:T(8,128)(2,1)S(1)} %get-tuple-element.7), channel_id=1, source_target_pairs={{0,1},{2,3},{4,5},{6,7},{8,9},{10,11},{12,13},{14,15},{16,17},{18,... | collective-permute-start | bytes 98312 | tf_op jit(solution)/shard_map/ppermute | solution.py:19
  128.8 1.3 collective-permute-start.5
  130.1 1.8 collective-permute-done.5
  132.0 3.0 %gather_fusion.2 = bf16[256,64,128]{2,1,0:T(8,128)(2,1)} fusion(bf16[64,36,128]{2,0,1:T(8,128)(2,1)S(1)} %copy_bitcast_fusion.1, s32[1024]{0:T(1024)S(1)} %pad_clamp_fusion), kind=kCustom, calls=%fused_computation.2 | custom fusion | bytes 8389632 | tf_op jit(solution)/shard_map/gather | solution.py:30
  135.1 7.7 %convolution_bitcast_fusion.1 = f32[32,8,8,128]{3,2,1,0:T(8,128)S(1)} fusion(bf16[64,32,8,128]{3,0,2,1:T(8,128)(2,1)} %bitcast.198, bf16[32,8,128,128]{3,2,1,0:T(8,128)(2,1)} %param.6), kind=kOutput, calls=%fused_computation.5 | convolution fusion | flops 536870912 | bytes 13631488 | tf_op jit(solution)/shard_map/rjab,krjb->kra/dot_general | solution.py:31
  142.8 0.5 fusion.24
  143.2 2.1 %collective-permute-start.6 = (bf16[64,256]{1,0:T(8,128)(2,1)S(1)}, bf16[64,256]{1,0:T(8,128)(2,1)S(1)}, u32[]{:S(2)}, u32[]{:S(2)}) collective-permute-start(bf16[64,256]{1,0:T(8,128)(2,1)S(1)} %get-tuple-element.5), channel_id=1, source_target_pairs={{0,1},{2,3},{4,5},{6,7},{8,9},{10,11},{12,13},{14,15},{16,17},{18,... | collective-permute-start | bytes 98312 | tf_op jit(solution)/shard_map/ppermute | solution.py:19
  145.3 1.5 collective-permute-start.7
  146.8 1.6 collective-permute-done.7
  148.6 3.0 %gather_fusion.3 = bf16[256,64,128]{2,1,0:T(8,128)(2,1)} fusion(bf16[64,36,128]{2,0,1:T(8,128)(2,1)S(1)} %copy_bitcast_fusion, s32[1024]{0:T(1024)S(1)} %pad_clamp_fusion), kind=kCustom, calls=%fused_computation.3 | custom fusion | bytes 8389632 | tf_op jit(solution)/shard_map/gather | solution.py:30
  151.6 7.7 %convolution_bitcast_fusion = f32[32,8,8,128]{3,2,1,0:T(8,128)S(1)} fusion(bf16[64,32,8,128]{3,0,2,1:T(8,128)(2,1)} %bitcast.195, bf16[32,8,128,128]{3,2,1,0:T(8,128)(2,1)} %param.6), kind=kOutput, calls=%fused_computation.4 | convolution fusion | flops 536870912 | bytes 13631488 | tf_op jit(solution)/shard_map/rjab,krjb->kra/dot_general | solution.py:31
  159.4 0.6 fusion.3
  160.2 19.1 %all_to_all.24 = bf16[16,64,256]{2,1,0:T(8,128)(2,1)S(1)} all-to-all(bf16[16,64,256]{2,1,0:T(8,128)(2,1)S(1)} %fusion.8), channel_id=1, replica_groups=mesh['vec'=16,'row'=2] {'vec'}, dimensions={0} | all-to-all | bytes 1048576 | tf_op jit(solution)/shard_map/all_to_all | solution.py:55
  179.3 1.0 copy.48
  (47 shorter events, 0.9 us)
Async XLA Ops:
  6.5 66.7 %copy-start = (bf16[1,256,1024]{2,1,0:T(8,128)(2,1)S(1)}, bf16[1,256,1024]{2,1,0:T(8,128)(2,1)}, u32[]{:S(2)}) copy-start(bf16[1,256,1024]{2,1,0:T(8,128)(2,1)} %param.4) | copy-start | bytes 1572868
  6.5 74.3 %copy-start.6 = (s32[32,8]{0,1:T(8,128)S(1)}, s32[32,8]{0,1:T(8,128)}, u32[]{:S(2)}) copy-start(s32[32,8]{0,1:T(8,128)} %param.7) | copy-start | bytes 3076
  6.5 66.7 %all-gather.2.cloned.1.call-start = ((), (), s32[]{:S(2)}) async-start(), calls=%async_computation.2 | async-start | bytes 2228224 | tf_op jit(solution)/shard_map/all_gather | solution.py:62
  76.4 18.6 %all-to-all-start = ((bf16[16,64,256]{2,1,0:T(8,128)(2,1)}), bf16[16,64,256]{2,1,0:T(8,128)(2,1)S(1)}, u32[]{:S(2)}, u32[]{:S(2)}) async-start(bf16[16,64,256]{2,1,0:T(8,128)(2,1)} %bitcast.1), calls=%async_computation | async-start | bytes 1048576 | tf_op jit(solution)/shard_map/all_to_all | solution.py:67
  95.0 2.6 %collective-permute-start = (bf16[64,256]{1,0:T(8,128)(2,1)S(1)}, bf16[64,256]{1,0:T(8,128)(2,1)S(1)}, u32[]{:S(2)}, u32[]{:S(2)}) collective-permute-start(bf16[64,256]{1,0:T(8,128)(2,1)S(1)} %get-tuple-element.11), channel_id=1, source_target_pairs={{0,1},{2,3},{4,5},{6,7},{8,9},{10,11},{12,13},{14,15},{16,17},{18,... | collective-permute-start | bytes 98312 | tf_op jit(solution)/shard_map/ppermute | solution.py:19
  96.3 3.1 %collective-permute-start.1 = (bf16[64,256]{1,0:T(8,128)(2,1)S(1)}, bf16[64,256]{1,0:T(8,128)(2,1)S(1)}, u32[]{:S(2)}, u32[]{:S(2)}) collective-permute-start(bf16[64,256]{1,0:T(8,128)(2,1)S(1)} %get-tuple-element.12), channel_id=1, source_target_pairs={{1,0},{3,2},{5,4},{7,6},{9,8},{11,10},{13,12},{15,14},{17,16},{19,... | collective-permute-start | bytes 98312 | tf_op jit(solution)/shard_map/ppermute | solution.py:22
  110.4 3.4 %collective-permute-start.2 = (bf16[64,256]{1,0:T(8,128)(2,1)S(1)}, bf16[64,256]{1,0:T(8,128)(2,1)S(1)}, u32[]{:S(2)}, u32[]{:S(2)}) collective-permute-start(bf16[64,256]{1,0:T(8,128)(2,1)S(1)} %get-tuple-element.9), channel_id=1, source_target_pairs={{0,1},{2,3},{4,5},{6,7},{8,9},{10,11},{12,13},{14,15},{16,17},{18,... | collective-permute-start | bytes 98312 | tf_op jit(solution)/shard_map/ppermute | solution.py:19
  112.5 3.1 %collective-permute-start.3 = (bf16[64,256]{1,0:T(8,128)(2,1)S(1)}, bf16[64,256]{1,0:T(8,128)(2,1)S(1)}, u32[]{:S(2)}, u32[]{:S(2)}) collective-permute-start(bf16[64,256]{1,0:T(8,128)(2,1)S(1)} %get-tuple-element.10), channel_id=1, source_target_pairs={{1,0},{3,2},{5,4},{7,6},{9,8},{11,10},{13,12},{15,14},{17,16},{19,... | collective-permute-start | bytes 98312 | tf_op jit(solution)/shard_map/ppermute | solution.py:22
  126.4 3.7 %copy-start.1 = (f32[32,8,8,128]{3,2,1,0:T(8,128)}, f32[32,8,8,128]{3,2,1,0:T(8,128)S(1)}, u32[]{:S(2)}) copy-start(f32[32,8,8,128]{3,2,1,0:T(8,128)S(1)} %convolution_bitcast_fusion.2) | copy-start | bytes 3145732
  126.7 3.4 %collective-permute-start.4 = (bf16[64,256]{1,0:T(8,128)(2,1)S(1)}, bf16[64,256]{1,0:T(8,128)(2,1)S(1)}, u32[]{:S(2)}, u32[]{:S(2)}) collective-permute-start(bf16[64,256]{1,0:T(8,128)(2,1)S(1)} %get-tuple-element.7), channel_id=1, source_target_pairs={{0,1},{2,3},{4,5},{6,7},{8,9},{10,11},{12,13},{14,15},{16,17},{18,... | collective-permute-start | bytes 98312 | tf_op jit(solution)/shard_map/ppermute | solution.py:19
  128.8 3.1 %collective-permute-start.5 = (bf16[64,256]{1,0:T(8,128)(2,1)S(1)}, bf16[64,256]{1,0:T(8,128)(2,1)S(1)}, u32[]{:S(2)}, u32[]{:S(2)}) collective-permute-start(bf16[64,256]{1,0:T(8,128)(2,1)S(1)} %get-tuple-element.8), channel_id=1, source_target_pairs={{1,0},{3,2},{5,4},{7,6},{9,8},{11,10},{13,12},{15,14},{17,16},{19,... | collective-permute-start | bytes 98312 | tf_op jit(solution)/shard_map/ppermute | solution.py:22
  135.1 7.7 %copy-start.2 = (f32[32,8,8,128]{3,2,1,0:T(8,128)S(1)}, f32[32,8,8,128]{3,2,1,0:T(8,128)}, u32[]{:S(2)}) copy-start(f32[32,8,8,128]{3,2,1,0:T(8,128)} %copy-done.1) | copy-start | bytes 3145732
  142.8 4.1 %copy-start.4 = (f32[32,8,8,128]{3,2,1,0:T(8,128)}, f32[32,8,8,128]{3,2,1,0:T(8,128)S(1)}, u32[]{:S(2)}) copy-start(f32[32,8,8,128]{3,2,1,0:T(8,128)S(1)} %convolution_bitcast_fusion.1) | copy-start | bytes 3145732
  143.2 3.6 %collective-permute-start.6 = (bf16[64,256]{1,0:T(8,128)(2,1)S(1)}, bf16[64,256]{1,0:T(8,128)(2,1)S(1)}, u32[]{:S(2)}, u32[]{:S(2)}) collective-permute-start(bf16[64,256]{1,0:T(8,128)(2,1)S(1)} %get-tuple-element.5), channel_id=1, source_target_pairs={{0,1},{2,3},{4,5},{6,7},{8,9},{10,11},{12,13},{14,15},{16,17},{18,... | collective-permute-start | bytes 98312 | tf_op jit(solution)/shard_map/ppermute | solution.py:19
  145.3 3.1 %collective-permute-start.7 = (bf16[64,256]{1,0:T(8,128)(2,1)S(1)}, bf16[64,256]{1,0:T(8,128)(2,1)S(1)}, u32[]{:S(2)}, u32[]{:S(2)}) collective-permute-start(bf16[64,256]{1,0:T(8,128)(2,1)S(1)} %get-tuple-element.6), channel_id=1, source_target_pairs={{1,0},{3,2},{5,4},{7,6},{9,8},{11,10},{13,12},{15,14},{17,16},{19,... | collective-permute-start | bytes 98312 | tf_op jit(solution)/shard_map/ppermute | solution.py:22
  151.6 7.7 %copy-start.3 = (f32[32,8,8,128]{3,2,1,0:T(8,128)S(1)}, f32[32,8,8,128]{3,2,1,0:T(8,128)}, u32[]{:S(2)}) copy-start(f32[32,8,8,128]{3,2,1,0:T(8,128)} %copy-done.1) | copy-start | bytes 3145732
  151.6 7.8 %copy-start.5 = (f32[32,8,8,128]{3,2,1,0:T(8,128)S(1)}, f32[32,8,8,128]{3,2,1,0:T(8,128)}, u32[]{:S(2)}) copy-start(f32[32,8,8,128]{3,2,1,0:T(8,128)} %copy-done.4) | copy-start | bytes 3145732
Sparse Core Ops, SparseCore 0:
  10.1 63.0 all-gather.1
